TPU v7x, 32 devices: a whole 2x2x4 slice. The times are simulated.
32 devices in a mesh: slab: 8 (over y, x, core), lat: 4 (over z).
Axes of the slice: x: 2, y: 2, z: 4, core: 2. Of those that a mesh axis runs over, the one named last changes fastest.
Arguments:
- tokens: bfloat16 [16, 16, 16, 1024], P(None, 'lat', 'slab'), may hold values from -6 to 6
- conv_first: float32 [27, 1024], replicated, may hold values from -1.25 to 1.25
- conv_second: float32 [27, 1024], replicated, may hold values from -1.25 to 1.25
- kv_weight: bfloat16 [2, 1024, 1024], P(None, None, 'lat'), may hold values from -0.1875 to 0.1875
- queries: bfloat16 [512, 1024], replicated, may hold values from -70 to 70
Outputs:
- decoded: bfloat16 [16, 16, 16, 1024], P(None, 'lat', 'slab')
All inputs are finite; a program needn't handle non-finite values.
Results may differ from a plain program's by a relative error of at most 0.012.
The roundings to bfloat16 on the way count: a program that leaves them out, or rounds other values in their place, can miss the bound.
Values may be sent and summed in bfloat16 or wider, within the bound.
No kernel may reach another device: no remote copies, remote signals or barrier semaphores. Data moves between devices by JAX's collectives and lax.ppermute only.
A program may use at most 64 MiB of HBM per device.

v0:
```python
import jax
import jax.numpy as jnp
from jax import lax
from jax.sharding import PartitionSpec as P


def with_halo(block, sides, width):
    for axis, dim in sides:
        count = lax.axis_size(axis)
        forward = [(i, i + 1) for i in range(count - 1)]
        backward = [(target, source) for source, target in forward]
        low = lax.ppermute(
            lax.slice_in_dim(block, block.shape[dim] - width, None, axis=dim), axis, forward
        )
        high = lax.ppermute(lax.slice_in_dim(block, 0, width, axis=dim), axis, backward)
        block = jnp.concatenate([low, block, high], axis=dim)
    return block


def conv_valid(padded, weights):
    size_x = padded.shape[0] - 2
    size_y = padded.shape[1] - 2
    size_z = padded.shape[2] - 2
    accum_sum = jnp.zeros((size_x, size_y, size_z, padded.shape[3]), jnp.float32)
    for tap_index in range(27):
        shift_x = tap_index // 9
        shift_y = tap_index // 3 % 3
        shift_z = tap_index % 3
        window = padded[
            shift_x : shift_x + size_x, shift_y : shift_y + size_y, shift_z : shift_z + size_z
        ]
        accum_sum = accum_sum + weights[tap_index] * window
    return accum_sum


def extend_first(field):
    return jnp.pad(field.astype(jnp.float32), ((1, 1), (0, 0), (0, 0), (0, 0)))


def local(tokens, conv_first, conv_second, kv_weight, queries):
    width = tokens.shape[3]
    source = tokens.astype(jnp.float32)
    padded_tokens = with_halo(tokens, (("slab", 2), ("lat", 1)), 1)
    inner_layer = jax.nn.gelu(conv_valid(extend_first(padded_tokens), conv_first)).astype(
        jnp.bfloat16
    )
    beside_all = with_halo(inner_layer, (("slab", 2), ("lat", 1)), 1)
    mixed = jax.nn.gelu(conv_valid(extend_first(beside_all), conv_second))
    hidden = (source + mixed).astype(jnp.bfloat16)
    token_rows = hidden.reshape(-1, width)
    product = jnp.einsum(
        "td,kdw->ktw",
        token_rows,
        lax.all_gather(kv_weight, "lat", axis=2, tiled=True),
        preferred_element_type=jnp.float32,
    )
    projected = product.astype(jnp.bfloat16)
    key_rows = projected[0]
    value_rows = projected[1]
    score_scale = 1.0 / width**0.5
    scores = (
        jnp.einsum("ld,td->lt", queries, key_rows, preferred_element_type=jnp.float32) * score_scale
    )
    local_max = jnp.max(scores, axis=1)
    maximum = lax.pmax(local_max, ("slab", "lat"))
    exponent = jnp.exp(scores - maximum[:, None])
    weights_bf = exponent.astype(jnp.bfloat16)
    denominator = jnp.sum(exponent, axis=1)
    numerator = jnp.dot(weights_bf, value_rows, preferred_element_type=jnp.float32)
    numer_total, denom_total = lax.psum((numerator, denominator), ("slab", "lat"))
    latents = (numer_total / denom_total[:, None]).astype(jnp.bfloat16)
    back = (
        jnp.einsum("td,ld->tl", token_rows, latents, preferred_element_type=jnp.float32)
        * score_scale
    )
    probs = jax.nn.softmax(back, axis=1).astype(jnp.bfloat16)
    result = token_rows.astype(jnp.float32) + jnp.dot(
        probs, latents, preferred_element_type=jnp.float32
    )
    return result.astype(jnp.bfloat16).reshape(hidden.shape)


def solution(mesh):
    placed = (P(None, "lat", "slab", None), P(), P(), P(None, None, "lat"), P())
    return jax.shard_map(
        local, mesh=mesh, in_specs=placed, out_specs=P(None, "lat", "slab", None), check_vma=False
    )
```

profile of v0, /device:TPU:0, one launch (start us, length us, event | category | flops | bytes accessed | tf_op | source)
XLA Modules:
  0.0 288.1 jit_solution(4803963372032662820)
XLA Ops:
  7.3 1.6 fusion.90
  8.9 2.4 collective-permute-start
  11.4 1.3 collective-permute-start.1
  12.7 4.1 %collective-permute-done.1 = bf16[16,4,1,1024]{3,2,1,0:T(2,128)(2,1)S(1)} collective-permute-done((bf16[16,4,1,1024]{3,2,1,0:T(2,128)(2,1)S(1)}, bf16[16,4,1,1024]{3,2,1,0:T(2,128)(2,1)S(1)}, u32[]{:S(2)}, u32[]{:S(2)}) %collective-permute-start.1) | collective-permute-done | bytes 131104 | tf_op jit(solution)/shard_map/ppermute | solution.py:15
  17.3 3.5 %collective-permute-start.2 = (bf16[16,1,4,1024]{3,2,1,0:T(4,128)(2,1)S(1)}, bf16[16,1,4,1024]{3,2,1,0:T(4,128)(2,1)S(1)}, u32[]{:S(2)}, u32[]{:S(2)}) collective-permute-start(bf16[16,1,4,1024]{3,2,1,0:T(4,128)(2,1)S(1)} %get-tuple-element.7), channel_id=1, source_target_pairs={{0,1},{1,2},{2,3},{4,5},{5,6},{6,7},{8,9},{9,10},{10,11},{12,13},{... | collective-permute-start | bytes 393224 | tf_op jit(solution)/shard_map/ppermute | solution.py:12
  20.8 1.3 collective-permute-start.3
  22.2 4.1 %collective-permute-done.2 = bf16[16,1,4,1024]{3,2,1,0:T(4,128)(2,1)S(1)} collective-permute-done((bf16[16,1,4,1024]{3,2,1,0:T(4,128)(2,1)S(1)}, bf16[16,1,4,1024]{3,2,1,0:T(4,128)(2,1)S(1)}, u32[]{:S(2)}, u32[]{:S(2)}) %collective-permute-start.2) | collective-permute-done | bytes 131104 | tf_op jit(solution)/shard_map/ppermute | solution.py:12
  26.2 5.3 %collective-permute-done.3 = bf16[16,1,4,1024]{3,2,1,0:T(4,128)(2,1)S(1)} collective-permute-done((bf16[16,1,4,1024]{3,2,1,0:T(4,128)(2,1)S(1)}, bf16[16,1,4,1024]{3,2,1,0:T(4,128)(2,1)S(1)}, u32[]{:S(2)}, u32[]{:S(2)}) %collective-permute-start.3) | collective-permute-done | bytes 131104 | tf_op jit(solution)/shard_map/ppermute | solution.py:15
  32.5 6.8 %fusion.79 = bf16[16,4,2,1024]{3,2,1,0:T(2,128)(2,1)S(1)} fusion(f32[16,6,4,1024]{3,2,1,0:T(4,128)S(1)} %maximum_convert_fusion, f32[1024]{0:T(1024)S(1)} %bitcast.122, f32[1024]{0:T(1024)S(1)} %bitcast.123, f32[1024]{0:T(1024)S(1)} %bitcast.98, f32[1024]{0:T(1024)S(1)} %bitcast.99, f32[1024]{0:T(1024)S(1)} %bitcast.100, f32[1024]{0:T(1024)S(1)} %bitcast.101, ...), kind=kLoop, calls=%fused_computation.126 | loop fusion | flops 8126464 | bytes 6664192 | tf_op jit(solution)/shard_map/convert_element_type | solution.py:44
  39.9 6.2 %collective-permute-start.4 = (bf16[16,4,1,1024]{3,2,1,0:T(2,128)(2,1)S(1)}, bf16[16,4,1,1024]{3,2,1,0:T(2,128)(2,1)S(1)}, u32[]{:S(2)}, u32[]{:S(2)}) collective-permute-start(bf16[16,4,1,1024]{3,2,1,0:T(2,128)(2,1)S(1)} %get-tuple-element.9), channel_id=1, source_target_pairs={{0,4},{4,8},{8,12},{12,16},{16,20},{20,24},{24,28},{1,5},{5,9},{9,... | collective-permute-start | bytes 393224 | tf_op jit(solution)/shard_map/ppermute | solution.py:12
  46.1 1.3 collective-permute-start.5
  47.5 2.7 collective-permute-done.5
  50.7 8.4 %collective-permute-start.6 = (bf16[16,1,4,1024]{3,2,1,0:T(4,128)(2,1)S(1)}, bf16[16,1,4,1024]{3,2,1,0:T(4,128)(2,1)S(1)}, u32[]{:S(2)}, u32[]{:S(2)}) collective-permute-start(bf16[16,1,4,1024]{3,2,1,0:T(4,128)(2,1)S(1)} %get-tuple-element.5), channel_id=1, source_target_pairs={{0,1},{1,2},{2,3},{4,5},{5,6},{6,7},{8,9},{9,10},{10,11},{12,13},{... | collective-permute-start | bytes 393224 | tf_op jit(solution)/shard_map/ppermute | solution.py:12
  59.1 1.3 collective-permute-start.7
  60.4 4.1 %collective-permute-done.6 = bf16[16,1,4,1024]{3,2,1,0:T(4,128)(2,1)S(1)} collective-permute-done((bf16[16,1,4,1024]{3,2,1,0:T(4,128)(2,1)S(1)}, bf16[16,1,4,1024]{3,2,1,0:T(4,128)(2,1)S(1)}, u32[]{:S(2)}, u32[]{:S(2)}) %collective-permute-start.6) | collective-permute-done | bytes 131104 | tf_op jit(solution)/shard_map/ppermute | solution.py:12
  64.5 12.2 %collective-permute-done.7 = bf16[16,1,4,1024]{3,2,1,0:T(4,128)(2,1)S(1)} collective-permute-done((bf16[16,1,4,1024]{3,2,1,0:T(4,128)(2,1)S(1)}, bf16[16,1,4,1024]{3,2,1,0:T(4,128)(2,1)S(1)}, u32[]{:S(2)}, u32[]{:S(2)}) %collective-permute-start.7) | collective-permute-done | bytes 131104 | tf_op jit(solution)/shard_map/ppermute | solution.py:15
  77.7 7.0 %fusion.80 = bf16[16,4,2,1024]{3,2,1,0:T(2,128)(2,1)S(1)} fusion(f32[16,6,4,1024]{3,2,1,0:T(4,128)S(1)} %maximum_convert_fusion.1, bf16[16,4,2,1024]{3,2,1,0:T(2,128)(2,1)S(1)} %copy-done.1, f32[1024]{0:T(1024)S(1)} %bitcast.95, f32[1024]{0:T(1024)S(1)} %bitcast.96, f32[1024]{0:T(1024)S(1)} %bitcast.71, f32[1024]{0:T(1024)S(1)} %bitcast.72, ...), kind=kLoop, calls=%fused_computation.127 | loop fusion | flops 8388608 | bytes 6926336 | tf_op jit(solution)/shard_map/convert_element_type | solution.py:49
  84.8 13.0 %all-gather.2.cloned.1.call-done = bf16[2,1024,1024]{2,1,0:T(8,128)(2,1)} async-done(((bf16[2,1024,256]{2,1,0:T(8,128)(2,1)}), bf16[2,1024,1024]{2,1,0:T(8,128)(2,1)}) %all-gather.2.cloned.1.call-update) | async-done | bytes 4194320 | tf_op jit(solution)/shard_map/all_gather | solution.py:54
  97.8 2.9 %fusion = bf16[2,128,1024]{2,1,0:T(8,128)(2,1)S(1)} fusion(bf16[128,1024,1]{1,0,2:T(8,128)(2,1)S(1)} %reshape.66, bf16[2,1024,1024]{2,1,0:T(8,128)(2,1)} %all-gather.2.cloned.1.call-done), kind=kOutput, calls=%fused_computation.3 | convolution fusion | flops 537133056 | bytes 4980736 | tf_op jit(solution)/shard_map/td,kdw->ktw/dot_general | solution.py:51
  101.2 39.5 %pmax.7 = f32[512]{0:T(512)S(1)} all-reduce(f32[512]{0:T(512)S(1)} %get-tuple-element.67), channel_id=1, replica_groups=mesh['slab'=8,'lat'=4] {'slab','lat'}, use_global_device_ids=true, to_apply=%region_1.2 | all-reduce | flops 512 | bytes 4096 | tf_op jit(solution)/shard_map/pmax | solution.py:65
  140.7 1.8 fusion.81
  142.6 40.4 %psum.15 = f32[512]{0:T(512)S(1)} all-reduce(f32[512]{0:T(512)S(1)} %fusion.82), channel_id=1, replica_groups=mesh['slab'=8,'lat'=4] {'slab','lat'}, use_global_device_ids=true, to_apply=%region_4.5 | all-reduce | flops 512 | bytes 4096 | tf_op jit(solution)/shard_map/psum | solution.py:70
  183.1 94.3 %all-reduce.4.cloned.1.call-done = f32[512,1024]{1,0:T(8,128)} async-done(((f32[512,1024]{1,0:T(8,128)}), f32[512,1024]{1,0:T(8,128)}) %all-reduce.4.cloned.1.call-update) | async-done | bytes 2097168 | tf_op jit(solution)/shard_map/psum | solution.py:70
  277.4 1.9 divide_convert_fusion
  (31 shorter events, 7.0 us)
Async XLA Ops:
  6.5 94.1 %copy-start = (bf16[512,1024]{1,0:T(8,128)(2,1)S(1)}, bf16[512,1024]{1,0:T(8,128)(2,1)}, u32[]{:S(2)}) copy-start(bf16[512,1024]{1,0:T(8,128)(2,1)} %param.9) | copy-start | bytes 3145732
  6.5 10.3 %copy-start.1 = (bf16[16,4,2,1024]{3,2,1,0:T(2,128)(2,1)S(1)}, bf16[16,4,2,1024]{3,2,1,0:T(2,128)(2,1)}, u32[]{:S(2)}) copy-start(bf16[16,4,2,1024]{3,2,1,0:T(2,128)(2,1)} %param.5) | copy-start | bytes 786436
  6.5 6.1 %copy-start.2 = (f32[27,1024]{1,0:T(8,128)S(1)}, f32[27,1024]{1,0:T(8,128)}, u32[]{:S(2)}) copy-start(f32[27,1024]{1,0:T(8,128)} %param.6) | copy-start | bytes 331780
  6.5 91.2 %all-gather.2.cloned.1.call-start = ((), (), s32[]{:S(2)}) async-start(), calls=%async_computation | async-start | bytes 5242880 | tf_op jit(solution)/shard_map/all_gather | solution.py:54
  7.3 270.1 %all-reduce.4.cloned.1.call-start = ((), (), s32[]{:S(2)}) async-start(), calls=%async_computation.1 | async-start | bytes 4194304 | tf_op jit(solution)/shard_map/psum | solution.py:70
  8.9 3.8 %collective-permute-start = (bf16[16,4,1,1024]{3,2,1,0:T(2,128)(2,1)S(1)}, bf16[16,4,1,1024]{3,2,1,0:T(2,128)(2,1)S(1)}, u32[]{:S(2)}, u32[]{:S(2)}) collective-permute-start(bf16[16,4,1,1024]{3,2,1,0:T(2,128)(2,1)S(1)} %get-tuple-element.11), channel_id=1, source_target_pairs={{0,4},{4,8},{8,12},{12,16},{16,20},{20,24},{24,28},{1,5},{5,9},{9,... | collective-permute-start | bytes 393224 | tf_op jit(solution)/shard_map/ppermute | solution.py:12
  11.4 5.5 %collective-permute-start.1 = (bf16[16,4,1,1024]{3,2,1,0:T(2,128)(2,1)S(1)}, bf16[16,4,1,1024]{3,2,1,0:T(2,128)(2,1)S(1)}, u32[]{:S(2)}, u32[]{:S(2)}) collective-permute-start(bf16[16,4,1,1024]{3,2,1,0:T(2,128)(2,1)S(1)} %get-tuple-element.12), channel_id=1, source_target_pairs={{4,0},{8,4},{12,8},{16,12},{20,16},{24,20},{28,24},{5,1},{9,5},{13... | collective-permute-start | bytes 393224 | tf_op jit(solution)/shard_map/ppermute | solution.py:15
  17.3 8.9 %collective-permute-start.2 = (bf16[16,1,4,1024]{3,2,1,0:T(4,128)(2,1)S(1)}, bf16[16,1,4,1024]{3,2,1,0:T(4,128)(2,1)S(1)}, u32[]{:S(2)}, u32[]{:S(2)}) collective-permute-start(bf16[16,1,4,1024]{3,2,1,0:T(4,128)(2,1)S(1)} %get-tuple-element.7), channel_id=1, source_target_pairs={{0,1},{1,2},{2,3},{4,5},{5,6},{6,7},{8,9},{9,10},{10,11},{12,13},{... | collective-permute-start | bytes 393224 | tf_op jit(solution)/shard_map/ppermute | solution.py:12
  20.8 10.7 %collective-permute-start.3 = (bf16[16,1,4,1024]{3,2,1,0:T(4,128)(2,1)S(1)}, bf16[16,1,4,1024]{3,2,1,0:T(4,128)(2,1)S(1)}, u32[]{:S(2)}, u32[]{:S(2)}) collective-permute-start(bf16[16,1,4,1024]{3,2,1,0:T(4,128)(2,1)S(1)} %get-tuple-element.8), channel_id=1, source_target_pairs={{1,0},{2,1},{3,2},{5,4},{6,5},{7,6},{9,8},{10,9},{11,10},{13,12},{... | collective-permute-start | bytes 393224 | tf_op jit(solution)/shard_map/ppermute | solution.py:15
  32.5 14.9 %copy-start.3 = (f32[27,1024]{1,0:T(8,128)S(1)}, f32[27,1024]{1,0:T(8,128)}, u32[]{:S(2)}) copy-start(f32[27,1024]{1,0:T(8,128)} %param.7) | copy-start | bytes 331780
  39.9 7.6 %collective-permute-start.4 = (bf16[16,4,1,1024]{3,2,1,0:T(2,128)(2,1)S(1)}, bf16[16,4,1,1024]{3,2,1,0:T(2,128)(2,1)S(1)}, u32[]{:S(2)}, u32[]{:S(2)}) collective-permute-start(bf16[16,4,1,1024]{3,2,1,0:T(2,128)(2,1)S(1)} %get-tuple-element.9), channel_id=1, source_target_pairs={{0,4},{4,8},{8,12},{12,16},{16,20},{20,24},{24,28},{1,5},{5,9},{9,... | collective-permute-start | bytes 393224 | tf_op jit(solution)/shard_map/ppermute | solution.py:12
  46.1 4.1 %collective-permute-start.5 = (bf16[16,4,1,1024]{3,2,1,0:T(2,128)(2,1)S(1)}, bf16[16,4,1,1024]{3,2,1,0:T(2,128)(2,1)S(1)}, u32[]{:S(2)}, u32[]{:S(2)}) collective-permute-start(bf16[16,4,1,1024]{3,2,1,0:T(2,128)(2,1)S(1)} %get-tuple-element.10), channel_id=1, source_target_pairs={{4,0},{8,4},{12,8},{16,12},{20,16},{24,20},{28,24},{5,1},{9,5},{13... | collective-permute-start | bytes 393224 | tf_op jit(solution)/shard_map/ppermute | solution.py:15
  50.7 13.8 %collective-permute-start.6 = (bf16[16,1,4,1024]{3,2,1,0:T(4,128)(2,1)S(1)}, bf16[16,1,4,1024]{3,2,1,0:T(4,128)(2,1)S(1)}, u32[]{:S(2)}, u32[]{:S(2)}) collective-permute-start(bf16[16,1,4,1024]{3,2,1,0:T(4,128)(2,1)S(1)} %get-tuple-element.5), channel_id=1, source_target_pairs={{0,1},{1,2},{2,3},{4,5},{5,6},{6,7},{8,9},{9,10},{10,11},{12,13},{... | collective-permute-start | bytes 393224 | tf_op jit(solution)/shard_map/ppermute | solution.py:12
  59.1 17.6 %collective-permute-start.7 = (bf16[16,1,4,1024]{3,2,1,0:T(4,128)(2,1)S(1)}, bf16[16,1,4,1024]{3,2,1,0:T(4,128)(2,1)S(1)}, u32[]{:S(2)}, u32[]{:S(2)}) collective-permute-start(bf16[16,1,4,1024]{3,2,1,0:T(4,128)(2,1)S(1)} %get-tuple-element.6), channel_id=1, source_target_pairs={{1,0},{2,1},{3,2},{5,4},{6,5},{7,6},{9,8},{10,9},{11,10},{13,12},{... | collective-permute-start | bytes 393224 | tf_op jit(solution)/shard_map/ppermute | solution.py:15
Sparse Core Ops, SparseCore 0:
  8.9 88.8 all-gather.1
  142.6 134.7 all-reduce.3
where the time goes:
time: 289 us; the launch traced here: 288 us
  waiting for transfers between devices  141 us (49%)
  blocking collectives  79.9 us (28%)
  starting transfers between devices  25.8 us (9%)
  other arithmetic  18.7 us (6%)
  between operations  13.6 us (5%)
  matrix products  6.15 us (2%)
  local copies, waits for them, and re-layouts  3.37 us (1%)
    psum x1, waiting for transfers between devices, local(): lax.psum((numerator, denominator), ('slab', 'lat'))  94.3 us
    psum x1, blocking collectives, local(): lax.psum((numerator, denominator), ('slab', 'lat'))  40.4 us
    pmax x1, blocking collectives, local(): maximum = lax.pmax(local_max, ('slab', 'lat'))  39.5 us
    ppermute x4, waiting for transfers between devices, with_halo(): lax.ppermute(lax.slice_in_dim(block, 0, width, axis=dim), axis, backward)  24.4 us
    ppermute x4, starting transfers between devices, with_halo(): lax.ppermute(lax.slice_in_dim(block, block.shape[dim] - width, None, axis...  20.5 us
    all_gather x1, waiting for transfers between devices, local(): lax.all_gather(kv_weight, 'lat', axis=2, tiled=True)  13 us
    ppermute x4, waiting for transfers between devices, with_halo(): lax.ppermute(lax.slice_in_dim(block, block.shape[dim] - width, None, axis...  8.15 us
    convert_element_type x1, other arithmetic, local(): hidden = (source + mixed).astype(jnp.bfloat16)  6.96 us
  transfers between devices with their start and end apart: 10, of which 8 were waited for; matrix products, arithmetic and copies ran while one was open for 7% of the time, Pallas kernels for 0%

commit v1 on v0

v1 whole, which is shorter than its diff:
```python
import functools

import jax
import jax.numpy as jnp
from jax import lax
from jax.experimental import pallas as pl
from jax.experimental.pallas import tpu as pltpu
from jax.sharding import PartitionSpec as P

F32 = jnp.float32
BF16 = jnp.bfloat16
LANES = 128
VMEM = pltpu.VMEM


def dot(a, b, contract):
    return lax.dot_general(a, b, (contract, ((), ())), preferred_element_type=F32)


def radices(count):
    found, stride = [], 1
    while stride < count:
        radix = 4 if count // stride % 4 == 0 else 2
        found.append((stride, radix))
        stride *= radix
    return found


def swap(block, axis, bits):
    count = lax.axis_size(axis)
    return lax.ppermute(block, axis, [(i, i ^ bits) for i in range(count)])


def gather_relative(block, axis, stages):
    for stride, radix in stages:
        received = [swap(block, axis, k * stride) for k in range(1, radix)]
        block = jnp.stack([block] + received)
    return block


def partner(position, count, near):
    other = position ^ 1 if near else ((position + 1) ^ 1) - 1
    return other if 0 <= other < count else None


def pair_exchange(block, axis, near):
    count = lax.axis_size(axis)
    pairs = [(partner(i, count, near), i) for i in range(count)]
    return lax.ppermute(block, axis, [p for p in pairs if p[0] is not None])


def conv_kernel(flags, own, near, far, near_rows, far_rows, first, second, out, cells, inner):
    size_y, size_z, size_x, _ = own.shape
    low_y, high_y, low_z, high_z = flags[0], flags[1], flags[2], flags[3]
    near_z, far_z, near_y, far_y = flags[4], flags[5], flags[6], flags[7]
    cells[2 : 2 + size_y, 2 : 2 + size_z] = own[...].astype(F32)
    cells[2 : 2 + size_y, pl.ds(near_z, 2)] = near[...].astype(F32)
    cells[2 : 2 + size_y, pl.ds(far_z, 2)] = far[...].astype(F32)
    for rows, start in ((near_rows, near_y), (far_rows, far_y)):
        cells[pl.ds(start, 2), 2 : 2 + size_z] = rows[0].astype(F32)
        cells[pl.ds(start, 2), pl.ds(near_z, 2)] = rows[1].astype(F32)
        cells[pl.ds(start, 2), pl.ds(far_z, 2)] = rows[2].astype(F32)

    def conv(source, weights, y, breadth):
        parts = [None, None, None]
        for b in range(3):
            for c in range(3):
                window = source[y + b, c : c + breadth]
                for a in range(3):
                    tap = 9 * a + 3 * b + c
                    term = weights[tap : tap + 1, :][None] * window
                    parts[a] = term if parts[a] is None else parts[a] + term
        place = lax.broadcasted_iota(jnp.int32, parts[0].shape, 1)
        before = jnp.where(place == 0, 0.0, pltpu.roll(parts[0], 1, 1))
        after = jnp.where(place == size_x - 1, 0.0, pltpu.roll(parts[2], size_x - 1, 1))
        return before + parts[1] + after

    for y in range(size_y + 2):
        value = jax.nn.gelu(conv(cells, first, y, size_z + 2)).astype(BF16).astype(F32)
        if y == 0:
            value = jnp.where(low_y > 0, value, 0.0)
        if y == size_y + 1:
            value = jnp.where(high_y > 0, value, 0.0)
        inner[y] = value
        inner[y, 0] = jnp.where(low_z > 0, inner[y, 0], 0.0)
        inner[y, size_z + 1] = jnp.where(high_z > 0, inner[y, size_z + 1], 0.0)
    for y in range(size_y):
        mixed = jax.nn.gelu(conv(inner, second, y, size_z))
        out[y] = (cells[y + 2, 2 : 2 + size_z] + mixed).astype(BF16)


def hidden_of(flags, own, pieces, first, second):
    size_y, size_z, size_x, width = own.shape
    lanes = LANES

    def spec(array):
        ahead = array.shape[:-1]
        return pl.BlockSpec(ahead + (lanes,), lambda i: (0,) * len(ahead) + (i,))

    weight_spec = pl.BlockSpec((first.shape[0], lanes), lambda i: (0, i))
    arrays = [own] + pieces
    return pl.pallas_call(
        conv_kernel,
        grid=(width // lanes,),
        out_shape=jax.ShapeDtypeStruct(own.shape, BF16),
        in_specs=[pl.BlockSpec(memory_space=pltpu.SMEM)]
        + [spec(a) for a in arrays]
        + [weight_spec, weight_spec],
        out_specs=spec(own),
        scratch_shapes=[
            VMEM((size_y + 4, size_z + 4, size_x, lanes), F32),
            VMEM((size_y + 2, size_z + 2, size_x, lanes), F32),
        ],
        compiler_params=pltpu.CompilerParams(vmem_limit_bytes=16 << 20),
        cost_estimate=pl.CostEstimate(flops=40_000_000, bytes_accessed=4 << 20, transcendentals=1 << 20),
        name="conv_pair",
    )(flags, *arrays, first, second)


def split_three(value):
    high = value.astype(BF16)
    rest = value - high.astype(F32)
    middle = rest.astype(BF16)
    low = (rest - middle.astype(F32)).astype(BF16)
    return high.astype(F32), middle.astype(F32), low.astype(F32)


def pack_columns(maximum, denominator):
    place = lax.broadcasted_iota(jnp.int32, (maximum.shape[0], LANES), 1)
    block = jnp.zeros((maximum.shape[0], LANES), F32)
    for lane, term in enumerate(split_three(maximum) + split_three(denominator)):
        block = jnp.where(place == lane, term, block)
    return block.astype(BF16)


def unpack_columns(block):
    place = lax.broadcasted_iota(jnp.int32, block.shape, 1)
    wide = block.astype(F32)

    def term(lane):
        return jnp.sum(jnp.where(place == lane, wide, 0.0), axis=1, keepdims=True)

    return term(0) + (term(1) + term(2)), term(3) + (term(4) + term(5))


def combine(blocks):
    width = blocks[0].shape[1] - LANES
    notes = [unpack_columns(b[:, width:]) for b in blocks]
    maximum = functools.reduce(jnp.maximum, [m for m, _ in notes])
    numerator, denominator = 0.0, 0.0
    for block, (own_max, own_denominator) in zip(blocks, notes):
        factor = jnp.exp(own_max - maximum)
        numerator = numerator + factor * block[:, :width].astype(F32)
        denominator = denominator + factor * own_denominator
    return numerator, maximum, denominator


def combine_kernel(*refs):
    out = refs[-1]
    numerator, maximum, denominator = combine([r[...] for r in refs[:-1]])
    width = numerator.shape[1]
    out[:, :width] = numerator.astype(BF16)
    out[:, width:] = pack_columns(maximum, denominator)


def mean_kernel(*refs):
    out = refs[-1]
    numerator, _, denominator = combine([r[...] for r in refs[:-1]])
    out[...] = (numerator / denominator).astype(BF16)


def small_call(kernel, arrays, shape, name, flops=0):
    count = sum(a.size for a in arrays)
    return pl.pallas_call(
        kernel,
        out_shape=jax.ShapeDtypeStruct(shape, BF16),
        in_specs=[pl.BlockSpec(memory_space=VMEM)] * len(arrays),
        out_specs=pl.BlockSpec(memory_space=VMEM),
        compiler_params=pltpu.CompilerParams(vmem_limit_bytes=24 << 20),
        cost_estimate=pl.CostEstimate(flops=flops + 4 * count, bytes_accessed=2 * count, transcendentals=0),
        name=name,
    )(*arrays)


def encode_kernel(score_scale, query, own, other, out):
    width = own.shape[1]
    queries = query[...]
    pieces = [own[...], other[...]]
    scores = [dot(queries, p, ((1,), (1,))) * score_scale for p in pieces]
    maximum = jnp.maximum(
        jnp.max(scores[0], axis=1, keepdims=True), jnp.max(scores[1], axis=1, keepdims=True)
    )
    exponents = [jnp.exp(s - maximum) for s in scores]
    denominator = sum(jnp.sum(e, axis=1, keepdims=True) for e in exponents)
    numerator = sum(dot(e.astype(BF16), p, ((1,), (0,))) for e, p in zip(exponents, pieces))
    out[:, :width] = numerator.astype(BF16)
    out[:, width:] = pack_columns(maximum, denominator)


def decode_kernel(score_scale, hidden, own, other, out):
    rows = hidden[...]
    pieces = [own[...], other[...]]
    back = [dot(rows, p, ((1,), (1,))) * score_scale for p in pieces]
    maximum = jnp.maximum(
        jnp.max(back[0], axis=1, keepdims=True), jnp.max(back[1], axis=1, keepdims=True)
    )
    exponents = [jnp.exp(b - maximum) for b in back]
    denominator = sum(jnp.sum(e, axis=1, keepdims=True) for e in exponents)
    result = rows.astype(F32)
    for exponent, piece in zip(exponents, pieces):
        result = result + dot((exponent / denominator).astype(BF16), piece, ((1,), (0,)))
    out[...] = result.astype(BF16)


def local(tokens, conv_first, conv_second, kv_weight, queries):
    size_x, size_y, size_z, width = tokens.shape
    slabs, lats = lax.axis_size("slab"), lax.axis_size("lat")
    slab, lat = lax.axis_index("slab"), lax.axis_index("lat")
    score_scale = 1.0 / width**0.5
    columns = kv_weight.shape[2]
    latents = queries.shape[0]
    block = latents // (slabs * lats)
    lat_stages = radices(lats)
    upper = [(2 * stride, radix) for stride, radix in radices(slabs // 2)]

    field = jnp.transpose(tokens, (1, 2, 0, 3))

    chunk = lats * block
    own_queries = lax.dynamic_slice(queries, (slab * chunk, lat * columns), (chunk, columns))
    partial = dot(own_queries, kv_weight[0], ((1,), (1,)))

    far = pair_exchange(field, "slab", False)
    near = pair_exchange(field, "slab", True)
    for stride, radix in lat_stages:
        sent = partial.astype(BF16)
        partial = partial + sum(
            swap(sent, "lat", k * stride).astype(F32) for k in range(1, radix)
        )
    even = lat % 2 == 0
    low = jnp.stack([field[:2], near[:2], far[:2]])
    high = jnp.stack([field[-2:], near[-2:], far[-2:]])
    near_rows = pair_exchange(jnp.where(even, high, low), "lat", True)
    far_rows = pair_exchange(jnp.where(even, low, high), "lat", False)
    key_queries = gather_relative(partial.astype(BF16), "slab", upper)
    key_queries = key_queries.reshape(latents // 2, width)

    parity = slab % 2
    edges = jnp.stack([lat > 0, lat < lats - 1, slab > 0, slab < slabs - 1]).astype(jnp.int32)
    places = jnp.stack(
        [
            jnp.where(parity == 0, size_z + 2, 0),
            jnp.where(parity == 0, 0, size_z + 2),
            jnp.where(even, size_y + 2, 0),
            jnp.where(even, 0, size_y + 2),
        ]
    ).astype(jnp.int32)
    flags = jnp.concatenate([edges, places])
    hidden = hidden_of(flags, field, [near, far, near_rows, far_rows], conv_first, conv_second)
    hidden = hidden.reshape(-1, width)
    other_hidden = swap(hidden, "slab", 1)

    half = width // 2
    value_half = lax.dynamic_slice_in_dim(kv_weight[1], parity * half, half, 0)
    value_mine = gather_relative(value_half, "lat", lat_stages).reshape(lats, half, columns)
    value_other = swap(value_mine, "slab", 1)

    payload = small_call(
        functools.partial(encode_kernel, score_scale),
        [key_queries, hidden, other_hidden],
        (latents // 2, width + LANES),
        "encode",
        4 * latents * hidden.shape[0] * width,
    )
    for stride, radix in reversed(upper):
        payload = payload.reshape(radix, -1, payload.shape[-1])
        blocks = [payload[0]] + [swap(payload[k], "slab", k * stride) for k in range(1, radix)]
        payload = small_call(combine_kernel, blocks, blocks[0].shape, "combine")
    for step, (stride, radix) in enumerate(lat_stages):
        blocks = [payload] + [swap(payload, "lat", k * stride) for k in range(1, radix)]
        if step < len(lat_stages) - 1:
            payload = small_call(combine_kernel, blocks, payload.shape, "combine")
        else:
            payload = small_call(mean_kernel, blocks, (chunk, width), "mean")
    mean_mine = lax.dynamic_slice_in_dim(payload, parity * half, half, 1)
    mean_other = lax.dynamic_slice_in_dim(payload, (1 - parity) * half, half, 1)
    projected = jnp.einsum("rd,jdw->rjw", mean_mine, value_mine, preferred_element_type=F32)
    projected = projected + jnp.einsum(
        "rd,jdw->rjw", mean_other, value_other, preferred_element_type=F32
    )
    bit = 1
    while bit < lats:
        paired = projected.reshape(chunk, lats // (2 * bit), 2, bit, columns)
        projected = jnp.where((lat & bit) > 0, paired[:, :, ::-1], paired).reshape(
            chunk, lats, columns
        )
        bit *= 2
    share = projected.astype(BF16).reshape(chunk, width)
    share = gather_relative(share, "slab", upper).reshape(latents // 2, width)
    other_share = swap(share, "slab", 1)

    result = small_call(
        functools.partial(decode_kernel, score_scale),
        [hidden, share, other_share],
        hidden.shape,
        "decode",
        4 * latents * hidden.shape[0] * width,
    )
    return jnp.transpose(result.reshape(field.shape), (2, 0, 1, 3))


def solution(mesh):
    placed = (P(None, "lat", "slab", None), P(), P(), P(None, None, "lat"), P())
    return jax.shard_map(
        local, mesh=mesh, in_specs=placed, out_specs=P(None, "lat", "slab", None), check_vma=False
    )
```

time: 289 us -> 97.7 us (0.34)
  waiting for transfers between devices: 141 us -> 42 us
  blocking collectives: 79.9 us -> 0 us
  other arithmetic: 18.7 us -> 3.51 us
  between operations: 13.6 us -> 0.24 us
  Pallas kernels: 0 us -> 8.97 us
  starting transfers between devices: 25.8 us -> 33.7 us
    psum x1 -> x0, waiting for transfers between devices: 94.3 us -> none  [local(): lax.psum((numerator, denominator), ('slab', 'lat'))]
    psum x1 -> x0, blocking collectives: 40.4 us -> none  [local(): lax.psum((numerator, denominator), ('slab', 'lat'))]
    pmax x1 -> x0, blocking collectives: 39.5 us -> none  [local(): maximum = lax.pmax(local_max, ('slab', 'lat'))]
    convert_element_type x5 -> x3, other arithmetic: 17.5 us -> 1.18 us  [the longest x1 1.08 us: local(): key_queries = gather_relative(partial.astype(BF16), 'slab', upper)]
    all_gather x1 -> x0, waiting for transfers between devices: 13 us -> none  [local(): lax.all_gather(kv_weight, 'lat', axis=2, tiled=True)]
    ppermute x8 -> x25, waiting for transfers between devices: 32.5 us -> 42 us  [the longest x21 34.3 us: swap(): return lax.ppermute(block, axis, [(i, i ^ bits) for i in range(count)])]
    pallas_call x0 -> x5, Pallas kernels: none -> 8.97 us  [the longest x1 6.43 us: hidden_of(): pl.pallas_call(conv_kernel, grid=(width // lanes,), out_shape=jax.ShapeDt...]
    ppermute x8 -> x25, starting transfers between devices: 25.7 us -> 33.7 us  [the longest x21 23.9 us: swap(): return lax.ppermute(block, axis, [(i, i ^ bits) for i in range(count)])]
  transfers between devices with their start and end apart: 10 -> 25, of which waited for: 8 -> 12; matrix products, arithmetic and copies ran while one was open for 7% -> 8% of each run, Pallas kernels for 0% -> 8%
where the time goes in v1:
time: 97.7 us; the launch traced here: 97.4 us
  waiting for transfers between devices  42 us (43%)
  starting transfers between devices  33.7 us (34%)
  Pallas kernels  8.97 us (9%)
  local copies, waits for them, and re-layouts  5.18 us (5%)
  matrix products  3.8 us (4%)
  other arithmetic  3.51 us (4%)
    ppermute x21, waiting for transfers between devices, swap(): return lax.ppermute(block, axis, [(i, i ^ bits) for i in range(count)])  34.3 us
    ppermute x21, starting transfers between devices, swap(): return lax.ppermute(block, axis, [(i, i ^ bits) for i in range(count)])  23.9 us
    ppermute x4, starting transfers between devices, pair_exchange(): return lax.ppermute(block, axis, [p for p in pairs if p[0] is not None])  9.73 us
    ppermute x4, waiting for transfers between devices, pair_exchange(): return lax.ppermute(block, axis, [p for p in pairs if p[0] is not None])  7.7 us
    pallas_call x1, Pallas kernels, hidden_of(): pl.pallas_call(conv_kernel, grid=(width // lanes,), out_shape=jax.ShapeDt...  6.43 us
    pallas_call x4, Pallas kernels, small_call(): pl.pallas_call(kernel, out_shape=jax.ShapeDtypeStruct(shape, BF16), in_sp...  2.54 us
    dot_general x1, matrix products, dot(): lax.dot_general(a, b, (contract, ((), ())), preferred_element_type=F32)  1.98 us
  transfers between devices with their start and end apart: 25, of which 12 were waited for; matrix products, arithmetic and copies ran while one was open for 8% of the time, Pallas kernels for 8%

profile of v1, /device:TPU:0, one launch (start us, length us, event | category | flops | bytes accessed | tf_op | source)
XLA Modules:
  0.0 97.4 jit_solution(5036095114892586108)
XLA Ops:
  1.9 4.4 %collective-permute-start = (bf16[4,2,16,1024]{3,2,1,0:T(8,128)(2,1)S(1)}, bf16[4,2,16,1024]{3,2,1,0:T(8,128)(2,1)S(1)}, u32[]{:S(2)}, u32[]{:S(2)}) collective-permute-start(bf16[4,2,16,1024]{3,2,1,0:T(8,128)(2,1)S(1)} %bitcast.63), channel_id=1, source_target_pairs={{4,0},{0,4},{12,8},{8,12},{20,16},{16,20},{28,24},{24,28},{5,1},{1... | collective-permute-start | bytes 786440 | tf_op jit(solution)/shard_map/ppermute | solution.py:49
  6.3 2.0 %fusion.14 = (bf16[64,1024]{1,0:T(8,128)(2,1)}, f32[64,1024]{1,0:T(8,128)S(1)}) fusion(bf16[2,1024,256]{2,1,0:T(8,128)(2,1)} %param.8, bf16[512,1024]{1,0:T(8,128)(2,1)S(1)} %copy-done, s32[]{:T(128)S(6)} %select_n.76, s32[]{:T(128)S(6)} %select_n.77), kind=kOutput, calls=%fused_computation.35 | convolution fusion | flops 33619968 | bytes 950280 | tf_op jit(solution)/shard_map/dot_general | solution.py:17
  8.2 3.6 %collective-permute-start.6 = (bf16[64,1024]{1,0:T(8,128)(2,1)}, bf16[64,1024]{1,0:T(8,128)(2,1)S(1)}, u32[]{:S(2)}, u32[]{:S(2)}) collective-permute-start(bf16[64,1024]{1,0:T(8,128)(2,1)} %get-tuple-element.17), channel_id=1, source_target_pairs={{0,3},{1,2},{2,1},{3,0},{4,7},{5,6},{6,5},{7,4},{8,11},{9,10},{10,... | collective-permute-start | bytes 393224 | tf_op jit(solution)/shard_map/ppermute | solution.py:31
  16.2 4.0 %collective-permute-start.2 = (bf16[3,2,2,16,1024]{4,3,2,1,0:T(8,128)(2,1)}, bf16[3,2,2,16,1024]{4,3,2,1,0:T(8,128)(2,1)S(1)}, u32[]{:S(2)}, u32[]{:S(2)}) collective-permute-start(bf16[3,2,2,16,1024]{4,3,2,1,0:T(8,128)(2,1)} %get-tuple-element.6), channel_id=1, source_target_pairs={{1,0},{0,1},{3,2},{2,3},{5,4},{4,5},{7,6},{6,7},{9,8},{8,9},{11,10... | collective-permute-start | bytes 1179656 | tf_op jit(solution)/shard_map/ppermute | solution.py:49
  20.9 1.5 %collective-permute-start.19 = (bf16[512,256]{1,0:T(8,128)(2,1)}, bf16[512,256]{1,0:T(8,128)(2,1)S(1)}, u32[]{:S(2)}, u32[]{:S(2)}) collective-permute-start(bf16[512,256]{1,0:T(8,128)(2,1)} %fusion.17), channel_id=1, source_target_pairs={{0,3},{1,2},{2,1},{3,0},{4,7},{5,6},{6,5},{7,4},{8,11},{9,10},{10,... | collective-permute-start | bytes 786440 | tf_op jit(solution)/shard_map/ppermute | solution.py:31
  22.4 2.0 %collective-permute-done.5 = bf16[64,1024]{1,0:T(8,128)(2,1)} collective-permute-done((bf16[64,1024]{1,0:T(8,128)(2,1)}, bf16[64,1024]{1,0:T(8,128)(2,1)}, u32[]{:S(2)}, u32[]{:S(2)}) %collective-permute-start.5) | collective-permute-done | bytes 131104 | tf_op jit(solution)/shard_map/ppermute | solution.py:31
  24.4 3.0 %collective-permute-start.17 = (bf16[512,256]{1,0:T(8,128)(2,1)}, bf16[512,256]{1,0:T(8,128)(2,1)}, u32[]{:S(2)}, u32[]{:S(2)}) collective-permute-start(bf16[512,256]{1,0:T(8,128)(2,1)} %fusion.17), channel_id=1, source_target_pairs={{0,1},{1,0},{2,3},{3,2},{4,5},{5,4},{6,7},{7,6},{8,9},{9,8},{10,11... | collective-permute-start | bytes 786440 | tf_op jit(solution)/shard_map/ppermute | solution.py:31
  29.7 7.7 %collective-permute-done.2.near_rows = bf16[3,2,2,16,1024]{4,3,2,1,0:T(8,128)(2,1)S(1)} collective-permute-done((bf16[3,2,2,16,1024]{4,3,2,1,0:T(8,128)(2,1)}, bf16[3,2,2,16,1024]{4,3,2,1,0:T(8,128)(2,1)S(1)}, u32[]{:S(2)}, u32[]{:S(2)}) %collective-permute-start.2) | collective-permute-done | bytes 393248 | tf_op jit(solution)/shard_map/ppermute | solution.py:49
  37.4 1.5 %collective-permute-start.8 = (bf16[64,1024]{1,0:T(8,128)(2,1)S(1)}, bf16[64,1024]{1,0:T(8,128)(2,1)S(1)}, u32[]{:S(2)}, u32[]{:S(2)}) collective-permute-start(bf16[64,1024]{1,0:T(8,128)(2,1)S(1)} %add_convert_fusion), channel_id=1, source_target_pairs={{0,16},{4,20},{8,24},{12,28},{16,0},{20,4},{24,8},{28,12},{1,17},{... | collective-permute-start | bytes 393224 | tf_op jit(solution)/shard_map/ppermute | solution.py:31
  38.9 6.4 %conv_pair.1 = bf16[4,2,16,1024]{3,2,1,0:T(8,128)(2,1)S(1)} custom-call(s32[8]{0:T(128)S(1)} %concatenate.3.flags, bf16[4,2,16,1024]{3,2,1,0:T(8,128)(2,1)S(1)} %bitcast.65, bf16[4,2,16,1024]{3,2,1,0:T(8,128)(2,1)S(1)} %collective-permute-done.near, bf16[4,2,16,1024]{3,2,1,0:T(8,128)(2,1)S(1)} %collective-permute-done.1.far, ...), custom_call_target="tpu_custom_call" | custom-call | flops 40000000 | bytes 4194304 | tf_op jit(solution)/shard_map/conv_pair/pallas_call | solution.py:102
  45.7 8.7 %collective-permute-done.18 = bf16[512,256]{1,0:T(8,128)(2,1)} collective-permute-done((bf16[512,256]{1,0:T(8,128)(2,1)}, bf16[512,256]{1,0:T(8,128)(2,1)}, u32[]{:S(2)}, u32[]{:S(2)}) %collective-permute-start.18) | collective-permute-done | bytes 262176 | tf_op jit(solution)/shard_map/ppermute | solution.py:31
  57.1 1.4 %collective-permute-start.13 = (bf16[64,1152]{1,0:T(8,128)(2,1)S(1)}, bf16[64,1152]{1,0:T(8,128)(2,1)S(1)}, u32[]{:S(2)}, u32[]{:S(2)}) collective-permute-start(bf16[64,1152]{1,0:T(8,128)(2,1)S(1)} %get-tuple-element.7), channel_id=1, source_target_pairs={{0,24},{4,28},{8,16},{12,20},{16,8},{20,12},{24,0},{28,4},{1,25},{... | collective-permute-start | bytes 442376 | tf_op jit(solution)/shard_map/ppermute | solution.py:31
  58.6 1.6 %collective-permute-start.12 = (bf16[64,1152]{1,0:T(8,128)(2,1)S(1)}, bf16[64,1152]{1,0:T(8,128)(2,1)S(1)}, u32[]{:S(2)}, u32[]{:S(2)}) collective-permute-start(bf16[64,1152]{1,0:T(8,128)(2,1)S(1)} %get-tuple-element.8), channel_id=1, source_target_pairs={{0,16},{4,20},{8,24},{12,28},{16,0},{20,4},{24,8},{28,12},{1,17},{... | collective-permute-start | bytes 442376 | tf_op jit(solution)/shard_map/ppermute | solution.py:31
  60.7 4.2 %collective-permute-done.13.refs_3_ = bf16[64,1152]{1,0:T(8,128)(2,1)S(1)} collective-permute-done((bf16[64,1152]{1,0:T(8,128)(2,1)S(1)}, bf16[64,1152]{1,0:T(8,128)(2,1)S(1)}, u32[]{:S(2)}, u32[]{:S(2)}) %collective-permute-start.13) | collective-permute-done | bytes 147488 | tf_op jit(solution)/shard_map/ppermute | solution.py:31
  64.9 2.2 %collective-permute-done.12.refs_2_ = bf16[64,1152]{1,0:T(8,128)(2,1)S(1)} collective-permute-done((bf16[64,1152]{1,0:T(8,128)(2,1)S(1)}, bf16[64,1152]{1,0:T(8,128)(2,1)S(1)}, u32[]{:S(2)}, u32[]{:S(2)}) %collective-permute-start.12) | collective-permute-done | bytes 147488 | tf_op jit(solution)/shard_map/ppermute | solution.py:31
  67.6 2.5 %collective-permute-start.16 = (bf16[64,1152]{1,0:T(8,128)(2,1)S(1)}, bf16[64,1152]{1,0:T(8,128)(2,1)S(1)}, u32[]{:S(2)}, u32[]{:S(2)}) collective-permute-start(bf16[64,1152]{1,0:T(8,128)(2,1)S(1)} %combine.1.refs_0_), channel_id=1, source_target_pairs={{0,3},{1,2},{2,1},{3,0},{4,7},{5,6},{6,5},{7,4},{8,11},{9,10},{10,... | collective-permute-start | bytes 442376 | tf_op jit(solution)/shard_map/ppermute | solution.py:31
  70.1 1.9 %collective-permute-start.14 = (bf16[64,1152]{1,0:T(8,128)(2,1)S(1)}, bf16[64,1152]{1,0:T(8,128)(2,1)S(1)}, u32[]{:S(2)}, u32[]{:S(2)}) collective-permute-start(bf16[64,1152]{1,0:T(8,128)(2,1)S(1)} %combine.1.refs_0_), channel_id=1, source_target_pairs={{0,1},{1,0},{2,3},{3,2},{4,5},{5,4},{6,7},{7,6},{8,9},{9,8},{10,11... | collective-permute-start | bytes 442376 | tf_op jit(solution)/shard_map/ppermute | solution.py:31
  72.0 4.2 %collective-permute-done.16.refs_3_ = bf16[64,1152]{1,0:T(8,128)(2,1)S(1)} collective-permute-done((bf16[64,1152]{1,0:T(8,128)(2,1)S(1)}, bf16[64,1152]{1,0:T(8,128)(2,1)S(1)}, u32[]{:S(2)}, u32[]{:S(2)}) %collective-permute-start.16) | collective-permute-done | bytes 147488 | tf_op jit(solution)/shard_map/ppermute | solution.py:31
  76.2 6.0 %collective-permute-done.15.refs_2_ = bf16[64,1152]{1,0:T(8,128)(2,1)S(1)} collective-permute-done((bf16[64,1152]{1,0:T(8,128)(2,1)S(1)}, bf16[64,1152]{1,0:T(8,128)(2,1)S(1)}, u32[]{:S(2)}, u32[]{:S(2)}) %collective-permute-start.15) | collective-permute-done | bytes 147488 | tf_op jit(solution)/shard_map/ppermute | solution.py:31
  82.6 1.5 %fusion.5 = f32[64,4,256]{2,0,1:T(8,128)S(1)} fusion(bf16[4,512,256]{2,1,0:T(8,128)(2,1)} %collective-permute-done.20, bf16[64,1024]{1,0:T(8,128)(2,1)S(1)} %mean.1, s32[]{:T(128)S(6)} %select_n.79), kind=kOutput, calls=%fused_computation.24 | convolution fusion | flops 67108864 | bytes 1376260 | tf_op jit(solution)/shard_map/rd,jdw->rjw/dot_general | solution.py:287
  84.8 1.5 %collective-permute-start.23 = (bf16[64,1024]{1,0:T(8,128)(2,1)S(1)}, bf16[64,1024]{1,0:T(8,128)(2,1)S(1)}, u32[]{:S(2)}, u32[]{:S(2)}) collective-permute-start(bf16[64,1024]{1,0:T(8,128)(2,1)S(1)} %convert_element_type.43), channel_id=1, source_target_pairs={{0,24},{4,28},{8,16},{12,20},{16,8},{20,12},{24,0},{28,4},{1,25},{... | collective-permute-start | bytes 393224 | tf_op jit(solution)/shard_map/ppermute | solution.py:31
  88.4 3.6 %collective-permute-done.23 = bf16[64,1024]{1,0:T(8,128)(2,1)S(1)} collective-permute-done((bf16[64,1024]{1,0:T(8,128)(2,1)S(1)}, bf16[64,1024]{1,0:T(8,128)(2,1)S(1)}, u32[]{:S(2)}, u32[]{:S(2)}) %collective-permute-start.23) | collective-permute-done | bytes 131104 | tf_op jit(solution)/shard_map/ppermute | solution.py:31
  92.0 1.4 %collective-permute-done.22 = bf16[64,1024]{1,0:T(8,128)(2,1)S(1)} collective-permute-done((bf16[64,1024]{1,0:T(8,128)(2,1)S(1)}, bf16[64,1024]{1,0:T(8,128)(2,1)S(1)}, u32[]{:S(2)}, u32[]{:S(2)}) %collective-permute-start.22) | collective-permute-done | bytes 131104 | tf_op jit(solution)/shard_map/ppermute | solution.py:31
  93.6 1.9 %collective-permute-done.24.other = bf16[256,1024]{1,0:T(8,128)(2,1)S(1)} collective-permute-done((bf16[256,1024]{1,0:T(8,128)(2,1)S(1)}, bf16[256,1024]{1,0:T(8,128)(2,1)S(1)}, u32[]{:S(2)}, u32[]{:S(2)}) %collective-permute-start.24) | collective-permute-done | bytes 524320 | tf_op jit(solution)/shard_map/ppermute | solution.py:31
  (63 shorter events, 18.4 us)
Async XLA Ops:
  1.2 13.3 %collective-permute-start.1 = (bf16[4,2,16,1024]{3,2,1,0:T(8,128)(2,1)S(1)}, bf16[4,2,16,1024]{3,2,1,0:T(8,128)(2,1)S(1)}, u32[]{:S(2)}, u32[]{:S(2)}) collective-permute-start(bf16[4,2,16,1024]{3,2,1,0:T(8,128)(2,1)S(1)} %bitcast.62), channel_id=1, source_target_pairs={{8,4},{4,8},{16,12},{12,16},{24,20},{20,24},{9,5},{5,9},{17,13},{1... | collective-permute-start | bytes 786440 | tf_op jit(solution)/shard_map/ppermute | solution.py:49
  1.9 12.6 %collective-permute-start = (bf16[4,2,16,1024]{3,2,1,0:T(8,128)(2,1)S(1)}, bf16[4,2,16,1024]{3,2,1,0:T(8,128)(2,1)S(1)}, u32[]{:S(2)}, u32[]{:S(2)}) collective-permute-start(bf16[4,2,16,1024]{3,2,1,0:T(8,128)(2,1)S(1)} %bitcast.63), channel_id=1, source_target_pairs={{4,0},{0,4},{12,8},{8,12},{20,16},{16,20},{28,24},{24,28},{5,1},{1... | collective-permute-start | bytes 786440 | tf_op jit(solution)/shard_map/ppermute | solution.py:49
  8.2 12.7 %collective-permute-start.6 = (bf16[64,1024]{1,0:T(8,128)(2,1)}, bf16[64,1024]{1,0:T(8,128)(2,1)S(1)}, u32[]{:S(2)}, u32[]{:S(2)}) collective-permute-start(bf16[64,1024]{1,0:T(8,128)(2,1)} %get-tuple-element.17), channel_id=1, source_target_pairs={{0,3},{1,2},{2,1},{3,0},{4,7},{5,6},{6,5},{7,4},{8,11},{9,10},{10,... | collective-permute-start | bytes 393224 | tf_op jit(solution)/shard_map/ppermute | solution.py:31
  11.8 12.5 %collective-permute-start.5 = (bf16[64,1024]{1,0:T(8,128)(2,1)}, bf16[64,1024]{1,0:T(8,128)(2,1)}, u32[]{:S(2)}, u32[]{:S(2)}) collective-permute-start(bf16[64,1024]{1,0:T(8,128)(2,1)} %get-tuple-element.17), channel_id=1, source_target_pairs={{0,2},{1,3},{2,0},{3,1},{4,6},{5,7},{6,4},{7,5},{8,10},{9,11},{10,... | collective-permute-start | bytes 393224 | tf_op jit(solution)/shard_map/ppermute | solution.py:31
  11.8 12.5 %collective-permute-start.4 = (bf16[64,1024]{1,0:T(8,128)(2,1)}, bf16[64,1024]{1,0:T(8,128)(2,1)}, u32[]{:S(2)}, u32[]{:S(2)}) collective-permute-start(bf16[64,1024]{1,0:T(8,128)(2,1)} %get-tuple-element.17), channel_id=1, source_target_pairs={{0,1},{1,0},{2,3},{3,2},{4,5},{5,4},{6,7},{7,6},{8,9},{9,8},{10,11... | collective-permute-start | bytes 393224 | tf_op jit(solution)/shard_map/ppermute | solution.py:31
  15.5 13.2 %collective-permute-start.3 = (bf16[3,2,2,16,1024]{4,3,2,1,0:T(8,128)(2,1)}, bf16[3,2,2,16,1024]{4,3,2,1,0:T(8,128)(2,1)S(1)}, u32[]{:S(2)}, u32[]{:S(2)}) collective-permute-start(bf16[3,2,2,16,1024]{4,3,2,1,0:T(8,128)(2,1)} %get-tuple-element.5), channel_id=1, source_target_pairs={{2,1},{1,2},{6,5},{5,6},{10,9},{9,10},{14,13},{13,14},{18,17},{17,... | collective-permute-start | bytes 1179656 | tf_op jit(solution)/shard_map/ppermute | solution.py:49
  16.2 21.1 %collective-permute-start.2 = (bf16[3,2,2,16,1024]{4,3,2,1,0:T(8,128)(2,1)}, bf16[3,2,2,16,1024]{4,3,2,1,0:T(8,128)(2,1)S(1)}, u32[]{:S(2)}, u32[]{:S(2)}) collective-permute-start(bf16[3,2,2,16,1024]{4,3,2,1,0:T(8,128)(2,1)} %get-tuple-element.6), channel_id=1, source_target_pairs={{1,0},{0,1},{3,2},{2,3},{5,4},{4,5},{7,6},{6,7},{9,8},{8,9},{11,10... | collective-permute-start | bytes 1179656 | tf_op jit(solution)/shard_map/ppermute | solution.py:49
  20.9 24.4 %collective-permute-start.19 = (bf16[512,256]{1,0:T(8,128)(2,1)}, bf16[512,256]{1,0:T(8,128)(2,1)S(1)}, u32[]{:S(2)}, u32[]{:S(2)}) collective-permute-start(bf16[512,256]{1,0:T(8,128)(2,1)} %fusion.17), channel_id=1, source_target_pairs={{0,3},{1,2},{2,1},{3,0},{4,7},{5,6},{6,5},{7,4},{8,11},{9,10},{10,... | collective-permute-start | bytes 786440 | tf_op jit(solution)/shard_map/ppermute | solution.py:31
  24.4 30.0 %collective-permute-start.18 = (bf16[512,256]{1,0:T(8,128)(2,1)}, bf16[512,256]{1,0:T(8,128)(2,1)}, u32[]{:S(2)}, u32[]{:S(2)}) collective-permute-start(bf16[512,256]{1,0:T(8,128)(2,1)} %fusion.17), channel_id=1, source_target_pairs={{0,2},{1,3},{2,0},{3,1},{4,6},{5,7},{6,4},{7,5},{8,10},{9,11},{10,... | collective-permute-start | bytes 786440 | tf_op jit(solution)/shard_map/ppermute | solution.py:31
  24.4 30.0 %collective-permute-start.17 = (bf16[512,256]{1,0:T(8,128)(2,1)}, bf16[512,256]{1,0:T(8,128)(2,1)}, u32[]{:S(2)}, u32[]{:S(2)}) collective-permute-start(bf16[512,256]{1,0:T(8,128)(2,1)} %fusion.17), channel_id=1, source_target_pairs={{0,1},{1,0},{2,3},{3,2},{4,5},{5,4},{6,7},{7,6},{8,9},{9,8},{10,11... | collective-permute-start | bytes 786440 | tf_op jit(solution)/shard_map/ppermute | solution.py:31
  28.7 27.4 %collective-permute-start.9 = (bf16[64,1024]{1,0:T(8,128)(2,1)S(1)}, bf16[64,1024]{1,0:T(8,128)(2,1)S(1)}, u32[]{:S(2)}, u32[]{:S(2)}) collective-permute-start(bf16[64,1024]{1,0:T(8,128)(2,1)S(1)} %add_convert_fusion), channel_id=1, source_target_pairs={{0,24},{4,28},{8,16},{12,20},{16,8},{20,12},{24,0},{28,4},{1,25},{... | collective-permute-start | bytes 393224 | tf_op jit(solution)/shard_map/ppermute | solution.py:31
  37.4 18.7 %collective-permute-start.8 = (bf16[64,1024]{1,0:T(8,128)(2,1)S(1)}, bf16[64,1024]{1,0:T(8,128)(2,1)S(1)}, u32[]{:S(2)}, u32[]{:S(2)}) collective-permute-start(bf16[64,1024]{1,0:T(8,128)(2,1)S(1)} %add_convert_fusion), channel_id=1, source_target_pairs={{0,16},{4,20},{8,24},{12,28},{16,0},{20,4},{24,8},{28,12},{1,17},{... | collective-permute-start | bytes 393224 | tf_op jit(solution)/shard_map/ppermute | solution.py:31
  45.3 10.8 %collective-permute-start.7 = (bf16[64,1024]{1,0:T(8,128)(2,1)S(1)}, bf16[64,1024]{1,0:T(8,128)(2,1)S(1)}, u32[]{:S(2)}, u32[]{:S(2)}) collective-permute-start(bf16[64,1024]{1,0:T(8,128)(2,1)S(1)} %add_convert_fusion), channel_id=1, source_target_pairs={{0,8},{4,12},{8,0},{12,4},{16,24},{20,28},{24,16},{28,20},{1,9},{5... | collective-permute-start | bytes 393224 | tf_op jit(solution)/shard_map/ppermute | solution.py:31
  55.5 27.1 %collective-permute-start.20 = (bf16[4,512,256]{2,1,0:T(8,128)(2,1)S(1)}, bf16[4,512,256]{2,1,0:T(8,128)(2,1)}, u32[]{:S(2)}, u32[]{:S(2)}) collective-permute-start(bf16[4,512,256]{2,1,0:T(8,128)(2,1)S(1)} %pad_maximum_fusion), channel_id=1, source_target_pairs={{0,4},{4,0},{8,12},{12,8},{16,20},{20,16},{24,28},{28,24},{1,5},{5... | collective-permute-start | bytes 3145736 | tf_op jit(solution)/shard_map/ppermute | solution.py:31
  57.1 7.7 %collective-permute-start.13 = (bf16[64,1152]{1,0:T(8,128)(2,1)S(1)}, bf16[64,1152]{1,0:T(8,128)(2,1)S(1)}, u32[]{:S(2)}, u32[]{:S(2)}) collective-permute-start(bf16[64,1152]{1,0:T(8,128)(2,1)S(1)} %get-tuple-element.7), channel_id=1, source_target_pairs={{0,24},{4,28},{8,16},{12,20},{16,8},{20,12},{24,0},{28,4},{1,25},{... | collective-permute-start | bytes 442376 | tf_op jit(solution)/shard_map/ppermute | solution.py:31
  58.6 8.5 %collective-permute-start.12 = (bf16[64,1152]{1,0:T(8,128)(2,1)S(1)}, bf16[64,1152]{1,0:T(8,128)(2,1)S(1)}, u32[]{:S(2)}, u32[]{:S(2)}) collective-permute-start(bf16[64,1152]{1,0:T(8,128)(2,1)S(1)} %get-tuple-element.8), channel_id=1, source_target_pairs={{0,16},{4,20},{8,24},{12,28},{16,0},{20,4},{24,8},{28,12},{1,17},{... | collective-permute-start | bytes 442376 | tf_op jit(solution)/shard_map/ppermute | solution.py:31
  60.2 7.0 %collective-permute-start.11 = (bf16[64,1152]{1,0:T(8,128)(2,1)S(1)}, bf16[64,1152]{1,0:T(8,128)(2,1)S(1)}, u32[]{:S(2)}, u32[]{:S(2)}) collective-permute-start(bf16[64,1152]{1,0:T(8,128)(2,1)S(1)} %get-tuple-element.9), channel_id=1, source_target_pairs={{0,8},{4,12},{8,0},{12,4},{16,24},{20,28},{24,16},{28,20},{1,9},{5... | collective-permute-start | bytes 442376 | tf_op jit(solution)/shard_map/ppermute | solution.py:31
  67.6 8.7 %collective-permute-start.16 = (bf16[64,1152]{1,0:T(8,128)(2,1)S(1)}, bf16[64,1152]{1,0:T(8,128)(2,1)S(1)}, u32[]{:S(2)}, u32[]{:S(2)}) collective-permute-start(bf16[64,1152]{1,0:T(8,128)(2,1)S(1)} %combine.1.refs_0_), channel_id=1, source_target_pairs={{0,3},{1,2},{2,1},{3,0},{4,7},{5,6},{6,5},{7,4},{8,11},{9,10},{10,... | collective-permute-start | bytes 442376 | tf_op jit(solution)/shard_map/ppermute | solution.py:31
  70.1 12.2 %collective-permute-start.15 = (bf16[64,1152]{1,0:T(8,128)(2,1)S(1)}, bf16[64,1152]{1,0:T(8,128)(2,1)S(1)}, u32[]{:S(2)}, u32[]{:S(2)}) collective-permute-start(bf16[64,1152]{1,0:T(8,128)(2,1)S(1)} %combine.1.refs_0_), channel_id=1, source_target_pairs={{0,2},{1,3},{2,0},{3,1},{4,6},{5,7},{6,4},{7,5},{8,10},{9,11},{10,... | collective-permute-start | bytes 442376 | tf_op jit(solution)/shard_map/ppermute | solution.py:31
  70.1 12.2 %collective-permute-start.14 = (bf16[64,1152]{1,0:T(8,128)(2,1)S(1)}, bf16[64,1152]{1,0:T(8,128)(2,1)S(1)}, u32[]{:S(2)}, u32[]{:S(2)}) collective-permute-start(bf16[64,1152]{1,0:T(8,128)(2,1)S(1)} %combine.1.refs_0_), channel_id=1, source_target_pairs={{0,1},{1,0},{2,3},{3,2},{4,5},{5,4},{6,7},{7,6},{8,9},{9,8},{10,11... | collective-permute-start | bytes 442376 | tf_op jit(solution)/shard_map/ppermute | solution.py:31
  84.8 7.2 %collective-permute-start.23 = (bf16[64,1024]{1,0:T(8,128)(2,1)S(1)}, bf16[64,1024]{1,0:T(8,128)(2,1)S(1)}, u32[]{:S(2)}, u32[]{:S(2)}) collective-permute-start(bf16[64,1024]{1,0:T(8,128)(2,1)S(1)} %convert_element_type.43), channel_id=1, source_target_pairs={{0,24},{4,28},{8,16},{12,20},{16,8},{20,12},{24,0},{28,4},{1,25},{... | collective-permute-start | bytes 393224 | tf_op jit(solution)/shard_map/ppermute | solution.py:31
  86.3 7.1 %collective-permute-start.22 = (bf16[64,1024]{1,0:T(8,128)(2,1)S(1)}, bf16[64,1024]{1,0:T(8,128)(2,1)S(1)}, u32[]{:S(2)}, u32[]{:S(2)}) collective-permute-start(bf16[64,1024]{1,0:T(8,128)(2,1)S(1)} %convert_element_type.43), channel_id=1, source_target_pairs={{0,16},{4,20},{8,24},{12,28},{16,0},{20,4},{24,8},{28,12},{1,17},{... | collective-permute-start | bytes 393224 | tf_op jit(solution)/shard_map/ppermute | solution.py:31
  87.3 6.1 %collective-permute-start.21 = (bf16[64,1024]{1,0:T(8,128)(2,1)S(1)}, bf16[64,1024]{1,0:T(8,128)(2,1)S(1)}, u32[]{:S(2)}, u32[]{:S(2)}) collective-permute-start(bf16[64,1024]{1,0:T(8,128)(2,1)S(1)} %convert_element_type.43), channel_id=1, source_target_pairs={{0,8},{4,12},{8,0},{12,4},{16,24},{20,28},{24,16},{28,20},{1,9},{5... | collective-permute-start | bytes 393224 | tf_op jit(solution)/shard_map/ppermute | solution.py:31
  93.5 2.0 %collective-permute-start.24 = (bf16[256,1024]{1,0:T(8,128)(2,1)S(1)}, bf16[256,1024]{1,0:T(8,128)(2,1)S(1)}, u32[]{:S(2)}, u32[]{:S(2)}) collective-permute-start(bf16[256,1024]{1,0:T(8,128)(2,1)S(1)} %bitcast.69), channel_id=1, source_target_pairs={{0,4},{4,0},{8,12},{12,8},{16,20},{20,16},{24,28},{28,24},{1,5},{5... | collective-permute-start | bytes 1572872 | tf_op jit(solution)/shard_map/ppermute | solution.py:31
  (5 other events, 56.4 us)
